TPU v7x, 32 devices: a whole 2x2x4 slice. The times are simulated.
32 devices in a mesh: groups: 2 (over y), tiles: 4 (over z), section: 4 (over x, core).
Axes of the slice: x: 2, y: 2, z: 4, core: 2. Of those that a mesh axis runs over, the one named last changes fastest.
Arguments:
- latents: float32 [4, 192, 8, 128], P('groups', None, 'tiles'), parts along dimension 0, may hold values from -6 to 6
- conv_weight: float32 [4, 27, 192, 192], P('section'), may hold values from -0.078125 to 0.078125
- gain: float32 [4, 192], P('section'), may hold values from 0.1 to 1.9
Outputs:
- decoded: float32 [4, 192, 8, 128], P('groups', 'section', 'tiles'), parts along dimension 0
There are 2 independent parts, one for each index of `groups`. A program takes and returns all parts, laid end to end along the dimension named above; an argument that names none is the same for every part. Nothing has to cross between parts.
All inputs are finite; a program needn't handle non-finite values.
Results may differ from a plain program's by a relative error of at most 0.00013.
Values sent between devices are 32-bit elements; how exact they have to be, the bound alone decides.
No kernel may reach another device: no remote copies, remote signals or barrier semaphores. Data moves between devices by JAX's collectives and lax.ppermute only.
A program may use at most 64 MiB of HBM per device.

v0:
```python
import jax
import jax.numpy as jnp
from jax import lax
from jax.sharding import PartitionSpec as P

EPSILON = 1e-06


def extended(block, sides, width):
    for axis, dim in sides:
        count = lax.axis_size(axis)
        forward = [(i, i + 1) for i in range(count - 1)]
        backward = [(target, source) for source, target in forward]
        low = lax.ppermute(
            lax.slice_in_dim(block, block.shape[dim] - width, None, axis=dim), axis, forward
        )
        high = lax.ppermute(lax.slice_in_dim(block, 0, width, axis=dim), axis, backward)
        block = jnp.concatenate([low, block, high], axis=dim)
    return block


def from_behind(value, axis, by):
    peers = lax.axis_size(axis)
    pairs = [(i, i + by) for i in range(peers) if 0 <= i + by < peers]
    return lax.ppermute(value, axis, pairs)


def broadcast(value, axis, source):
    kept = jnp.where(lax.axis_index(axis) == source, value, 0).astype(value.dtype)
    return lax.psum(kept, axis)


def normalize(values, gain_row):
    meansq = jnp.mean(values * values, axis=1, keepdims=True)
    scaled = values * lax.rsqrt(meansq + EPSILON) * gain_row[None, :, None, None]
    return jax.nn.silu(scaled)


def add_rim(normed):
    return extended(normed, (("tiles", 2),), 1)


def convolve(padded, kernel, block_len, rows_here, col_count):
    summed = jnp.zeros((block_len, kernel.shape[1], rows_here, col_count), jnp.float32)
    for time_off in range(3):
        for row_off in range(3):
            for col_off in range(3):
                window = padded[
                    time_off : time_off + block_len,
                    :,
                    row_off : row_off + rows_here,
                    col_off : col_off + col_count,
                ]
                summed = summed + jnp.einsum(
                    "oi,tirw->torw",
                    kernel[time_off * 9 + row_off * 3 + col_off],
                    window,
                    precision=lax.Precision.HIGHEST,
                )
    return summed


def by_layers(latents, conv_weight, gain):
    kernel = conv_weight[0]
    gain_row = gain[0]
    frame_count, channels, rows_here, col_count = latents.shape
    layer_count = lax.axis_size("section")
    position = lax.axis_index("section")
    block_count = frame_count // frame_count
    step_count = block_count + layer_count - 1
    initial = jnp.zeros((frame_count, channels, rows_here, col_count), jnp.float32)
    memory_init = jnp.zeros((2, channels, rows_here + 2, col_count), jnp.float32)
    results_init = jnp.zeros_like(latents)

    def compute(operand):
        return convolve(operand, kernel, frame_count, rows_here, col_count)

    def skipped(operand):
        return jnp.zeros((frame_count, channels, rows_here, col_count), jnp.float32)

    def advance(step_now, loop_state):
        passing, memory, results = loop_state
        incoming = from_behind(passing, "section", 1)
        block_index = step_now - position
        active = (block_index >= 0) & (block_index < block_count)
        source = jnp.where(position == 0, latents, incoming)
        normed = normalize(source, gain_row)
        with_rim = add_rim(normed)
        joined = jnp.concatenate([memory, with_rim], axis=0)
        padded = jnp.pad(joined, ((0, 0), (0, 0), (0, 0), (1, 1)))
        branch = lax.cond(active, compute, skipped, padded)
        output = source + branch
        memory = jnp.where(active, joined[-2:], memory)
        store_now = active & (position == layer_count - 1)
        results = jnp.where(store_now, output, results)
        return (output, memory, results)

    final_state = lax.fori_loop(0, step_count, advance, (initial, memory_init, results_init))
    gathered = broadcast(final_state[2], "section", layer_count - 1)
    share = channels // layer_count
    return lax.dynamic_slice_in_dim(gathered, position * share, share, 1)


def local(latents, conv_weight, gain):
    return by_layers(latents, conv_weight, gain)


def solution(mesh):
    return jax.shard_map(
        local,
        mesh=mesh,
        in_specs=(
            P("groups", None, "tiles", None),
            P("section", None, None, None),
            P("section", None),
        ),
        out_specs=P("groups", "section", "tiles", None),
        check_vma=False,
    )
```

profile of v0, /device:TPU:0, one launch (start us, length us, event | category | flops | bytes accessed | tf_op | source)
XLA Modules:
  0.0 192.6 jit_solution(15802440383919716907)
XLA Ops:
  6.5 1.0 copy.4
  7.6 99.6 %while.20 = (s32[]{:T(128)}, f32[2,192,2,128]{3,1,2,0:T(8,128)S(1)}, f32[2,192,4,128]{3,1,2,0:T(8,128)S(1)}, f32[2,192,2,128]{3,1,2,0:T(8,128)S(1)}, pred[]{:T(5...) while((s32[]{:T(128)}, ...), condition=%wide.region_4.5_spmd.clone, body=%wide.region_0.4_spmd.clone.sunk | while | flops 6121095680 | bytes 99492952 | solution.py:98
  7.6 2.4 %collective-permute-start = (f32[2,192,2,128]{3,1,2,0:T(8,128)S(1)}, f32[2,192,2,128]{3,1,2,0:T(8,128)S(1)}, u32[]{:S(2)}, u32[]{:S(2)}) collective-permute-start(f32[2,192,2,128]{3,1,2,0:T(8,128)S(1)} %broadcast_select_fusion.6), channel_id=1, source_target_pairs={{0,1},{1,2},{2,3},{4,5},{5,6},{6,7},{8,9},{9,10},{10,11},{12,13},{... | collective-permute-start | bytes 1179656 | tf_op jit(solution)/shard_map/while/body/eval_jaxpr/ppermute | solution.py:25
  10.0 1.3 collective-permute-done
  11.4 0.9 divide_multiply_fusion.2
  12.3 1.3 collective-permute-start.1
  13.6 4.9 %collective-permute-start.2 = (f32[2,192,1,128]{3,1,2,0:T(8,128)S(1)}, f32[2,192,1,128]{3,1,2,0:T(8,128)S(1)}, u32[]{:S(2)}, u32[]{:S(2)}) collective-permute-start(f32[2,192,1,128]{3,1,2,0:T(8,128)S(1)} %get-tuple-element.376), channel_id=1, source_target_pairs={{0,4},{4,8},{8,12},{1,5},{5,9},{9,13},{2,6},{6,10},{10,14},{3,7},{... | collective-permute-start | bytes 589832 | tf_op jit(solution)/shard_map/while/body/eval_jaxpr/ppermute | solution.py:14
  18.6 1.7 collective-permute-done.1
  20.3 1.5 collective-permute-done.2
  21.7 0.2 maximum_select_fusion.2
  22.1 19.5 %conditional.3 = (f32[2,192,2,128]{3,1,2,0:T(8,128)S(1)}) conditional(s32[]{:T(128)} %convert_element_type.22, () %tuple.63, (f32[4,192,4,128]{3,1,2,0:T(8,128)S(1)}, f32[27,192,192]{2,1,0:T(8,128)}) %tuple.64), branch_computations={%region_2.2_spmd, %region_3.3_spmd} | conditional | flops 6117851136 | bytes 84541480 | solution.py:91
  22.1 1.6 fusion.46
  23.8 1.6 convolution_add_fusion.10
  25.4 1.6 convolution_add_fusion.9
  26.9 0.5 fusion.42
  27.5 0.7 fusion.7
  28.1 0.6 convolution_add_fusion.7
  28.8 0.5 fusion.38
  29.3 0.7 fusion.8
  30.0 0.6 convolution_add_fusion.5
  30.6 0.5 fusion.34
  31.2 0.7 fusion.9
  31.8 0.6 convolution_add_fusion.3
  32.5 0.5 fusion.30
  33.0 0.7 fusion.10
  33.7 0.6 convolution_add_fusion.1
  34.3 0.5 fusion.26
  34.9 0.7 fusion.12
  35.5 0.6 fusion
  36.2 0.6 fusion.1
  36.8 0.5 fusion.13
  37.3 0.6 fusion.2
  38.0 0.6 fusion.3
  38.6 0.5 fusion.14
  39.2 0.6 fusion.4
  39.8 0.6 fusion.5
  40.4 0.5 fusion.15
  41.0 0.6 fusion.6
  41.9 1.3 collective-permute-start
  43.2 1.3 collective-permute-done
  44.6 0.9 divide_multiply_fusion.2
  45.5 1.3 collective-permute-start.1
  46.8 5.0 %collective-permute-start.2 = (f32[2,192,1,128]{3,1,2,0:T(8,128)S(1)}, f32[2,192,1,128]{3,1,2,0:T(8,128)S(1)}, u32[]{:S(2)}, u32[]{:S(2)}) collective-permute-start(f32[2,192,1,128]{3,1,2,0:T(8,128)S(1)} %get-tuple-element.376), channel_id=1, source_target_pairs={{0,4},{4,8},{8,12},{1,5},{5,9},{9,13},{2,6},{6,10},{10,14},{3,7},{... | collective-permute-start | bytes 589832 | tf_op jit(solution)/shard_map/while/body/eval_jaxpr/ppermute | solution.py:14
  51.8 3.5 %collective-permute-done.1 = f32[2,192,1,128]{3,1,2,0:T(8,128)S(1)} collective-permute-done((f32[2,192,1,128]{3,1,2,0:T(8,128)S(1)}, f32[2,192,1,128]{3,1,2,0:T(8,128)S(1)}, u32[]{:S(2)}, u32[]{:S(2)}) %collective-permute-start.1) | collective-permute-done | bytes 196640 | tf_op jit(solution)/shard_map/while/body/eval_jaxpr/ppermute | solution.py:17
  55.3 1.2 collective-permute-done.2
  56.5 0.2 maximum_select_fusion.2
  57.2 20.9 %collective-permute-start = (f32[2,192,2,128]{3,1,2,0:T(8,128)S(1)}, f32[2,192,2,128]{3,1,2,0:T(8,128)S(1)}, u32[]{:S(2)}, u32[]{:S(2)}) collective-permute-start(f32[2,192,2,128]{3,1,2,0:T(8,128)S(1)} %broadcast_select_fusion.6), channel_id=1, source_target_pairs={{0,1},{1,2},{2,3},{4,5},{5,6},{6,7},{8,9},{9,10},{10,11},{12,13},{... | collective-permute-start | bytes 1179656 | tf_op jit(solution)/shard_map/while/body/eval_jaxpr/ppermute | solution.py:25
  78.1 1.3 collective-permute-done
  79.5 0.9 divide_multiply_fusion.2
  80.4 1.3 collective-permute-start.1
  81.7 5.0 %collective-permute-start.2 = (f32[2,192,1,128]{3,1,2,0:T(8,128)S(1)}, f32[2,192,1,128]{3,1,2,0:T(8,128)S(1)}, u32[]{:S(2)}, u32[]{:S(2)}) collective-permute-start(f32[2,192,1,128]{3,1,2,0:T(8,128)S(1)} %get-tuple-element.376), channel_id=1, source_target_pairs={{0,4},{4,8},{8,12},{1,5},{5,9},{9,13},{2,6},{6,10},{10,14},{3,7},{... | collective-permute-start | bytes 589832 | tf_op jit(solution)/shard_map/while/body/eval_jaxpr/ppermute | solution.py:14
  86.7 1.7 collective-permute-done.1
  88.4 1.5 collective-permute-done.2
  89.8 0.2 maximum_select_fusion.2
  90.5 4.5 %collective-permute-start = (f32[2,192,2,128]{3,1,2,0:T(8,128)S(1)}, f32[2,192,2,128]{3,1,2,0:T(8,128)S(1)}, u32[]{:S(2)}, u32[]{:S(2)}) collective-permute-start(f32[2,192,2,128]{3,1,2,0:T(8,128)S(1)} %broadcast_select_fusion.6), channel_id=1, source_target_pairs={{0,1},{1,2},{2,3},{4,5},{5,6},{6,7},{8,9},{9,10},{10,11},{12,13},{... | collective-permute-start | bytes 1179656 | tf_op jit(solution)/shard_map/while/body/eval_jaxpr/ppermute | solution.py:25
  95.0 1.3 collective-permute-done
  96.4 0.9 divide_multiply_fusion.2
  97.3 1.3 collective-permute-start.1
  98.6 4.7 %collective-permute-start.2 = (f32[2,192,1,128]{3,1,2,0:T(8,128)S(1)}, f32[2,192,1,128]{3,1,2,0:T(8,128)S(1)}, u32[]{:S(2)}, u32[]{:S(2)}) collective-permute-start(f32[2,192,1,128]{3,1,2,0:T(8,128)S(1)} %get-tuple-element.376), channel_id=1, source_target_pairs={{0,4},{4,8},{8,12},{1,5},{5,9},{9,13},{2,6},{6,10},{10,14},{3,7},{... | collective-permute-start | bytes 589832 | tf_op jit(solution)/shard_map/while/body/eval_jaxpr/ppermute | solution.py:14
  103.3 1.7 collective-permute-done.1
  105.0 1.5 collective-permute-done.2
  107.1 1.1 copy_select_fusion
  108.3 76.0 %all-reduce.3.cloned.1.call-done = f32[2,192,2,128]{3,2,1,0:T(2,128)} async-done(((f32[2,192,2,128]{3,2,1,0:T(2,128)}), f32[2,192,2,128]{3,2,1,0:T(2,128)}) %all-reduce.3.cloned.1.call-update) | async-done | bytes 393232 | tf_op jit(solution)/shard_map/psum | solution.py:30
  184.2 1.5 constant_dynamic-slice_fusion
  (38 shorter events, 2.3 us)
Async XLA Ops:
  6.5 177.7 %all-reduce.3.cloned.1.call-start = ((), (), s32[]{:S(2)}) async-start(), calls=%async_computation | async-start | bytes 786432 | tf_op jit(solution)/shard_map/psum | solution.py:30
  7.6 3.7 %collective-permute-start = (f32[2,192,2,128]{3,1,2,0:T(8,128)S(1)}, f32[2,192,2,128]{3,1,2,0:T(8,128)S(1)}, u32[]{:S(2)}, u32[]{:S(2)}) collective-permute-start(f32[2,192,2,128]{3,1,2,0:T(8,128)S(1)} %broadcast_select_fusion.6), channel_id=1, source_target_pairs={{0,1},{1,2},{2,3},{4,5},{5,6},{6,7},{8,9},{9,10},{10,11},{12,13},{... | collective-permute-start | bytes 1179656 | tf_op jit(solution)/shard_map/while/body/eval_jaxpr/ppermute | solution.py:25
  12.3 7.9 %collective-permute-start.1 = (f32[2,192,1,128]{3,1,2,0:T(8,128)S(1)}, f32[2,192,1,128]{3,1,2,0:T(8,128)S(1)}, u32[]{:S(2)}, u32[]{:S(2)}) collective-permute-start(f32[2,192,1,128]{3,1,2,0:T(8,128)S(1)} %get-tuple-element.375), channel_id=1, source_target_pairs={{4,0},{8,4},{12,8},{5,1},{9,5},{13,9},{6,2},{10,6},{14,10},{7,3},{... | collective-permute-start | bytes 589832 | tf_op jit(solution)/shard_map/while/body/eval_jaxpr/ppermute | solution.py:17
  13.6 8.1 %collective-permute-start.2 = (f32[2,192,1,128]{3,1,2,0:T(8,128)S(1)}, f32[2,192,1,128]{3,1,2,0:T(8,128)S(1)}, u32[]{:S(2)}, u32[]{:S(2)}) collective-permute-start(f32[2,192,1,128]{3,1,2,0:T(8,128)S(1)} %get-tuple-element.376), channel_id=1, source_target_pairs={{0,4},{4,8},{8,12},{1,5},{5,9},{9,13},{2,6},{6,10},{10,14},{3,7},{... | collective-permute-start | bytes 589832 | tf_op jit(solution)/shard_map/while/body/eval_jaxpr/ppermute | solution.py:14
  22.1 4.8 %copy-start = (f32[27,192,192]{2,1,0:T(8,128)S(1)}, f32[27,192,192]{2,1,0:T(8,128)}, u32[]{:S(2)}) copy-start(f32[27,192,192]{2,1,0:T(8,128)} %get-tuple-element.219) | copy-start | bytes 11943940 | tf_op jit(solution)/shard_map/while/body/eval_jaxpr/cond
  41.9 2.6 %collective-permute-start = (f32[2,192,2,128]{3,1,2,0:T(8,128)S(1)}, f32[2,192,2,128]{3,1,2,0:T(8,128)S(1)}, u32[]{:S(2)}, u32[]{:S(2)}) collective-permute-start(f32[2,192,2,128]{3,1,2,0:T(8,128)S(1)} %broadcast_select_fusion.6), channel_id=1, source_target_pairs={{0,1},{1,2},{2,3},{4,5},{5,6},{6,7},{8,9},{9,10},{10,11},{12,13},{... | collective-permute-start | bytes 1179656 | tf_op jit(solution)/shard_map/while/body/eval_jaxpr/ppermute | solution.py:25
  45.5 9.8 %collective-permute-start.1 = (f32[2,192,1,128]{3,1,2,0:T(8,128)S(1)}, f32[2,192,1,128]{3,1,2,0:T(8,128)S(1)}, u32[]{:S(2)}, u32[]{:S(2)}) collective-permute-start(f32[2,192,1,128]{3,1,2,0:T(8,128)S(1)} %get-tuple-element.375), channel_id=1, source_target_pairs={{4,0},{8,4},{12,8},{5,1},{9,5},{13,9},{6,2},{10,6},{14,10},{7,3},{... | collective-permute-start | bytes 589832 | tf_op jit(solution)/shard_map/while/body/eval_jaxpr/ppermute | solution.py:17
  46.8 9.7 %collective-permute-start.2 = (f32[2,192,1,128]{3,1,2,0:T(8,128)S(1)}, f32[2,192,1,128]{3,1,2,0:T(8,128)S(1)}, u32[]{:S(2)}, u32[]{:S(2)}) collective-permute-start(f32[2,192,1,128]{3,1,2,0:T(8,128)S(1)} %get-tuple-element.376), channel_id=1, source_target_pairs={{0,4},{4,8},{8,12},{1,5},{5,9},{9,13},{2,6},{6,10},{10,14},{3,7},{... | collective-permute-start | bytes 589832 | tf_op jit(solution)/shard_map/while/body/eval_jaxpr/ppermute | solution.py:14
  57.2 22.2 %collective-permute-start = (f32[2,192,2,128]{3,1,2,0:T(8,128)S(1)}, f32[2,192,2,128]{3,1,2,0:T(8,128)S(1)}, u32[]{:S(2)}, u32[]{:S(2)}) collective-permute-start(f32[2,192,2,128]{3,1,2,0:T(8,128)S(1)} %broadcast_select_fusion.6), channel_id=1, source_target_pairs={{0,1},{1,2},{2,3},{4,5},{5,6},{6,7},{8,9},{9,10},{10,11},{12,13},{... | collective-permute-start | bytes 1179656 | tf_op jit(solution)/shard_map/while/body/eval_jaxpr/ppermute | solution.py:25
  80.4 8.0 %collective-permute-start.1 = (f32[2,192,1,128]{3,1,2,0:T(8,128)S(1)}, f32[2,192,1,128]{3,1,2,0:T(8,128)S(1)}, u32[]{:S(2)}, u32[]{:S(2)}) collective-permute-start(f32[2,192,1,128]{3,1,2,0:T(8,128)S(1)} %get-tuple-element.375), channel_id=1, source_target_pairs={{4,0},{8,4},{12,8},{5,1},{9,5},{13,9},{6,2},{10,6},{14,10},{7,3},{... | collective-permute-start | bytes 589832 | tf_op jit(solution)/shard_map/while/body/eval_jaxpr/ppermute | solution.py:17
  81.7 8.2 %collective-permute-start.2 = (f32[2,192,1,128]{3,1,2,0:T(8,128)S(1)}, f32[2,192,1,128]{3,1,2,0:T(8,128)S(1)}, u32[]{:S(2)}, u32[]{:S(2)}) collective-permute-start(f32[2,192,1,128]{3,1,2,0:T(8,128)S(1)} %get-tuple-element.376), channel_id=1, source_target_pairs={{0,4},{4,8},{8,12},{1,5},{5,9},{9,13},{2,6},{6,10},{10,14},{3,7},{... | collective-permute-start | bytes 589832 | tf_op jit(solution)/shard_map/while/body/eval_jaxpr/ppermute | solution.py:14
  90.5 5.8 %collective-permute-start = (f32[2,192,2,128]{3,1,2,0:T(8,128)S(1)}, f32[2,192,2,128]{3,1,2,0:T(8,128)S(1)}, u32[]{:S(2)}, u32[]{:S(2)}) collective-permute-start(f32[2,192,2,128]{3,1,2,0:T(8,128)S(1)} %broadcast_select_fusion.6), channel_id=1, source_target_pairs={{0,1},{1,2},{2,3},{4,5},{5,6},{6,7},{8,9},{9,10},{10,11},{12,13},{... | collective-permute-start | bytes 1179656 | tf_op jit(solution)/shard_map/while/body/eval_jaxpr/ppermute | solution.py:25
  97.3 7.7 %collective-permute-start.1 = (f32[2,192,1,128]{3,1,2,0:T(8,128)S(1)}, f32[2,192,1,128]{3,1,2,0:T(8,128)S(1)}, u32[]{:S(2)}, u32[]{:S(2)}) collective-permute-start(f32[2,192,1,128]{3,1,2,0:T(8,128)S(1)} %get-tuple-element.375), channel_id=1, source_target_pairs={{4,0},{8,4},{12,8},{5,1},{9,5},{13,9},{6,2},{10,6},{14,10},{7,3},{... | collective-permute-start | bytes 589832 | tf_op jit(solution)/shard_map/while/body/eval_jaxpr/ppermute | solution.py:17
  98.6 7.9 %collective-permute-start.2 = (f32[2,192,1,128]{3,1,2,0:T(8,128)S(1)}, f32[2,192,1,128]{3,1,2,0:T(8,128)S(1)}, u32[]{:S(2)}, u32[]{:S(2)}) collective-permute-start(f32[2,192,1,128]{3,1,2,0:T(8,128)S(1)} %get-tuple-element.376), channel_id=1, source_target_pairs={{0,4},{4,8},{8,12},{1,5},{5,9},{9,13},{2,6},{6,10},{10,14},{3,7},{... | collective-permute-start | bytes 589832 | tf_op jit(solution)/shard_map/while/body/eval_jaxpr/ppermute | solution.py:14
Sparse Core Ops, SparseCore 0:
  108.4 75.7 all-reduce.2
where the time goes:
time: 193 us
  waiting for transfers between devices  95.3 us (49%)
  starting transfers between devices  54 us (28%)
  matrix products  19.3 us (10%)
  between operations  13.4 us (7%)
  other arithmetic  7.2 us (4%)
  local copies, waits for them, and re-layouts  2.76 us (1%)
    psum x1, waiting for transfers between devices, broadcast(): return lax.psum(kept, axis)  76 us
    ppermute x4, starting transfers between devices, from_behind(): return lax.ppermute(value, axis, pairs)  29.1 us
    ppermute x4, starting transfers between devices, extended(): lax.ppermute(lax.slice_in_dim(block, block.shape[dim] - width, None, axis...  19.7 us
    dot_general x27, matrix products, convolve(): jnp.einsum('oi,tirw->torw', kernel[time_off * 9 + row_off * 3 + col_off],...  19.3 us
    ppermute x4, waiting for transfers between devices, extended(): lax.ppermute(lax.slice_in_dim(block, 0, width, axis=dim), axis, backward)  8.53 us
    ppermute x4, waiting for transfers between devices, extended(): lax.ppermute(lax.slice_in_dim(block, block.shape[dim] - width, None, axis...  5.56 us
    ppermute x4, waiting for transfers between devices, from_behind(): return lax.ppermute(value, axis, pairs)  5.23 us
    ppermute x4, starting transfers between devices, extended(): lax.ppermute(lax.slice_in_dim(block, 0, width, axis=dim), axis, backward)  5.17 us
  transfers between devices with their start and end apart: 13, of which 13 were waited for; matrix products, arithmetic and copies ran while one was open for 0% of the time, Pallas kernels for 0%

commit v1 on v0

--- a/solution.py
+++ b/solution.py
@@ -27,7 +27,7 @@
 
 def broadcast(value, axis, source):
     kept = jnp.where(lax.axis_index(axis) == source, value, 0).astype(value.dtype)
-    return lax.psum(kept, axis)
+    return jnp.sum(lax.all_gather(kept, axis), axis=0)
 
 
 def normalize(values, gain_row):

time: 193 us -> 180 us (0.933)
  waiting for transfers between devices: 95.3 us -> 81.9 us
    psum x1 -> x0, waiting for transfers between devices: 76 us -> none  [broadcast(): return lax.psum(kept, axis)]
    all_gather x0 -> x1, waiting for transfers between devices: none -> 62.6 us  [broadcast(): return jnp.sum(lax.all_gather(kept, axis), axis=0)]
where the time goes in v1:
time: 180 us; the launch traced here: 179 us
  waiting for transfers between devices  81.9 us (46%)
  starting transfers between devices  53.9 us (30%)
  matrix products  19.1 us (11%)
  between operations  13.4 us (7%)
  other arithmetic  8.44 us (5%)
  local copies, waits for them, and re-layouts  1.93 us (1%)
    all_gather x1, waiting for transfers between devices, broadcast(): return jnp.sum(lax.all_gather(kept, axis), axis=0)  62.6 us
    ppermute x4, starting transfers between devices, from_behind(): return lax.ppermute(value, axis, pairs)  29 us
    ppermute x4, starting transfers between devices, extended(): lax.ppermute(lax.slice_in_dim(block, block.shape[dim] - width, None, axis...  19.7 us
    dot_general x27, matrix products, convolve(): jnp.einsum('oi,tirw->torw', kernel[time_off * 9 + row_off * 3 + col_off],...  19.1 us
    ppermute x4, waiting for transfers between devices, extended(): lax.ppermute(lax.slice_in_dim(block, 0, width, axis=dim), axis, backward)  8.53 us
    ppermute x4, waiting for transfers between devices, extended(): lax.ppermute(lax.slice_in_dim(block, block.shape[dim] - width, None, axis...  5.56 us
    ppermute x4, waiting for transfers between devices, from_behind(): return lax.ppermute(value, axis, pairs)  5.23 us
    ppermute x4, starting transfers between devices, extended(): lax.ppermute(lax.slice_in_dim(block, 0, width, axis=dim), axis, backward)  5.17 us
  transfers between devices with their start and end apart: 13, of which 13 were waited for; matrix products, arithmetic and copies ran while one was open for 0% of the time, Pallas kernels for 0%

profile of v1, /device:TPU:0, one launch (start us, length us, event | category | flops | bytes accessed | tf_op | source)
XLA Modules:
  0.0 179.4 jit_solution(15946517350453860792)
XLA Ops:
  6.5 1.0 copy.5
  7.6 99.4 %while.20 = (s32[]{:T(128)}, f32[2,192,2,128]{3,1,2,0:T(8,128)S(1)}, f32[2,192,4,128]{3,1,2,0:T(8,128)S(1)}, f32[2,192,2,128]{3,1,2,0:T(8,128)S(1)}, pred[]{:T(5...) while((s32[]{:T(128)}, ...), condition=%wide.region_4.5_spmd.clone, body=%wide.region_0.4_spmd.clone.sunk | while | flops 6121095680 | bytes 99492952 | solution.py:98
  7.6 2.4 %collective-permute-start = (f32[2,192,2,128]{3,1,2,0:T(8,128)S(1)}, f32[2,192,2,128]{3,1,2,0:T(8,128)S(1)}, u32[]{:S(2)}, u32[]{:S(2)}) collective-permute-start(f32[2,192,2,128]{3,1,2,0:T(8,128)S(1)} %broadcast_select_fusion.7), channel_id=1, source_target_pairs={{0,1},{1,2},{2,3},{4,5},{5,6},{6,7},{8,9},{9,10},{10,11},{12,13},{... | collective-permute-start | bytes 1179656 | tf_op jit(solution)/shard_map/while/body/eval_jaxpr/ppermute | solution.py:25
  10.0 1.3 collective-permute-done
  11.4 0.9 divide_multiply_fusion.2
  12.3 1.3 collective-permute-start.1
  13.6 4.9 %collective-permute-start.2 = (f32[2,192,1,128]{3,1,2,0:T(8,128)S(1)}, f32[2,192,1,128]{3,1,2,0:T(8,128)S(1)}, u32[]{:S(2)}, u32[]{:S(2)}) collective-permute-start(f32[2,192,1,128]{3,1,2,0:T(8,128)S(1)} %get-tuple-element.386), channel_id=1, source_target_pairs={{0,4},{4,8},{8,12},{1,5},{5,9},{9,13},{2,6},{6,10},{10,14},{3,7},{... | collective-permute-start | bytes 589832 | tf_op jit(solution)/shard_map/while/body/eval_jaxpr/ppermute | solution.py:14
  18.6 1.7 collective-permute-done.1
  20.3 1.5 collective-permute-done.2
  22.1 19.4 %conditional.3 = (f32[2,192,2,128]{3,1,2,0:T(8,128)S(1)}) conditional(s32[]{:T(128)} %convert_element_type.22, () %tuple.64, (f32[4,192,4,128]{3,1,2,0:T(8,128)S(1)}, f32[27,192,192]{2,1,0:T(8,128)}) %tuple.65), branch_computations={%region_2.2_spmd, %region_3.3_spmd} | conditional | flops 6117851136 | bytes 84541480 | solution.py:91
  22.2 1.6 fusion.46
  23.8 1.6 convolution_add_fusion.10
  25.4 1.6 convolution_add_fusion.9
  26.9 0.5 fusion.42
  27.5 0.7 fusion.7
  28.1 0.6 convolution_add_fusion.7
  28.8 0.5 fusion.38
  29.3 0.7 fusion.8
  30.0 0.6 convolution_add_fusion.5
  30.6 0.5 fusion.34
  31.1 0.7 fusion.9
  31.8 0.6 convolution_add_fusion.3
  32.4 0.5 fusion.30
  33.0 0.7 fusion.10
  33.6 0.6 convolution_add_fusion.1
  34.3 0.5 fusion.26
  34.8 0.6 fusion.12
  35.4 0.6 fusion
  36.1 0.6 fusion.1
  36.7 0.5 fusion.13
  37.2 0.6 fusion.2
  37.9 0.6 fusion.3
  38.5 0.5 fusion.14
  39.1 0.6 fusion.4
  39.7 0.6 fusion.5
  40.3 0.5 fusion.15
  40.9 0.6 fusion.6
  41.8 1.3 collective-permute-start
  43.1 1.3 collective-permute-done
  44.5 0.9 divide_multiply_fusion.2
  45.4 1.3 collective-permute-start.1
  46.7 5.0 %collective-permute-start.2 = (f32[2,192,1,128]{3,1,2,0:T(8,128)S(1)}, f32[2,192,1,128]{3,1,2,0:T(8,128)S(1)}, u32[]{:S(2)}, u32[]{:S(2)}) collective-permute-start(f32[2,192,1,128]{3,1,2,0:T(8,128)S(1)} %get-tuple-element.386), channel_id=1, source_target_pairs={{0,4},{4,8},{8,12},{1,5},{5,9},{9,13},{2,6},{6,10},{10,14},{3,7},{... | collective-permute-start | bytes 589832 | tf_op jit(solution)/shard_map/while/body/eval_jaxpr/ppermute | solution.py:14
  51.7 3.5 %collective-permute-done.1 = f32[2,192,1,128]{3,1,2,0:T(8,128)S(1)} collective-permute-done((f32[2,192,1,128]{3,1,2,0:T(8,128)S(1)}, f32[2,192,1,128]{3,1,2,0:T(8,128)S(1)}, u32[]{:S(2)}, u32[]{:S(2)}) %collective-permute-start.1) | collective-permute-done | bytes 196640 | tf_op jit(solution)/shard_map/while/body/eval_jaxpr/ppermute | solution.py:17
  55.2 1.2 collective-permute-done.2
  56.4 0.2 maximum_select_fusion.2
  57.1 20.8 %collective-permute-start = (f32[2,192,2,128]{3,1,2,0:T(8,128)S(1)}, f32[2,192,2,128]{3,1,2,0:T(8,128)S(1)}, u32[]{:S(2)}, u32[]{:S(2)}) collective-permute-start(f32[2,192,2,128]{3,1,2,0:T(8,128)S(1)} %broadcast_select_fusion.7), channel_id=1, source_target_pairs={{0,1},{1,2},{2,3},{4,5},{5,6},{6,7},{8,9},{9,10},{10,11},{12,13},{... | collective-permute-start | bytes 1179656 | tf_op jit(solution)/shard_map/while/body/eval_jaxpr/ppermute | solution.py:25
  77.9 1.3 collective-permute-done
  79.3 0.9 divide_multiply_fusion.2
  80.2 1.3 collective-permute-start.1
  81.5 5.0 %collective-permute-start.2 = (f32[2,192,1,128]{3,1,2,0:T(8,128)S(1)}, f32[2,192,1,128]{3,1,2,0:T(8,128)S(1)}, u32[]{:S(2)}, u32[]{:S(2)}) collective-permute-start(f32[2,192,1,128]{3,1,2,0:T(8,128)S(1)} %get-tuple-element.386), channel_id=1, source_target_pairs={{0,4},{4,8},{8,12},{1,5},{5,9},{9,13},{2,6},{6,10},{10,14},{3,7},{... | collective-permute-start | bytes 589832 | tf_op jit(solution)/shard_map/while/body/eval_jaxpr/ppermute | solution.py:14
  86.5 1.7 collective-permute-done.1
  88.2 1.5 collective-permute-done.2
  89.7 0.2 maximum_select_fusion.2
  90.4 4.5 %collective-permute-start = (f32[2,192,2,128]{3,1,2,0:T(8,128)S(1)}, f32[2,192,2,128]{3,1,2,0:T(8,128)S(1)}, u32[]{:S(2)}, u32[]{:S(2)}) collective-permute-start(f32[2,192,2,128]{3,1,2,0:T(8,128)S(1)} %broadcast_select_fusion.7), channel_id=1, source_target_pairs={{0,1},{1,2},{2,3},{4,5},{5,6},{6,7},{8,9},{9,10},{10,11},{12,13},{... | collective-permute-start | bytes 1179656 | tf_op jit(solution)/shard_map/while/body/eval_jaxpr/ppermute | solution.py:25
  94.8 1.3 collective-permute-done
  96.2 0.9 divide_multiply_fusion.2
  97.1 1.3 collective-permute-start.1
  98.4 4.7 %collective-permute-start.2 = (f32[2,192,1,128]{3,1,2,0:T(8,128)S(1)}, f32[2,192,1,128]{3,1,2,0:T(8,128)S(1)}, u32[]{:S(2)}, u32[]{:S(2)}) collective-permute-start(f32[2,192,1,128]{3,1,2,0:T(8,128)S(1)} %get-tuple-element.386), channel_id=1, source_target_pairs={{0,4},{4,8},{8,12},{1,5},{5,9},{9,13},{2,6},{6,10},{10,14},{3,7},{... | collective-permute-start | bytes 589832 | tf_op jit(solution)/shard_map/while/body/eval_jaxpr/ppermute | solution.py:14
  103.2 1.7 collective-permute-done.1
  104.8 1.5 collective-permute-done.2
  107.0 0.8 broadcast_select_fusion.3
  107.8 62.6 %all-gather.3.cloned.1.call-done = f32[8,192,2,128]{3,1,2,0:T(8,128)} async-done(((f32[2,192,2,128]{3,1,2,0:T(8,128)}), f32[8,192,2,128]{3,1,2,0:T(8,128)}) %all-gather.3.cloned.1.call-update) | async-done | bytes 1572880 | tf_op jit(solution)/shard_map/all_gather | solution.py:30
  170.3 1.5 reduce_sum.25
  171.9 0.7 copy.6
  (40 shorter events, 2.6 us)
Async XLA Ops:
  6.5 163.8 %all-gather.3.cloned.1.call-start = ((), (), s32[]{:S(2)}) async-start(), calls=%async_computation | async-start | bytes 1966080 | tf_op jit(solution)/shard_map/all_gather | solution.py:30
  7.6 3.7 %collective-permute-start = (f32[2,192,2,128]{3,1,2,0:T(8,128)S(1)}, f32[2,192,2,128]{3,1,2,0:T(8,128)S(1)}, u32[]{:S(2)}, u32[]{:S(2)}) collective-permute-start(f32[2,192,2,128]{3,1,2,0:T(8,128)S(1)} %broadcast_select_fusion.7), channel_id=1, source_target_pairs={{0,1},{1,2},{2,3},{4,5},{5,6},{6,7},{8,9},{9,10},{10,11},{12,13},{... | collective-permute-start | bytes 1179656 | tf_op jit(solution)/shard_map/while/body/eval_jaxpr/ppermute | solution.py:25
  12.3 7.9 %collective-permute-start.1 = (f32[2,192,1,128]{3,1,2,0:T(8,128)S(1)}, f32[2,192,1,128]{3,1,2,0:T(8,128)S(1)}, u32[]{:S(2)}, u32[]{:S(2)}) collective-permute-start(f32[2,192,1,128]{3,1,2,0:T(8,128)S(1)} %get-tuple-element.385), channel_id=1, source_target_pairs={{4,0},{8,4},{12,8},{5,1},{9,5},{13,9},{6,2},{10,6},{14,10},{7,3},{... | collective-permute-start | bytes 589832 | tf_op jit(solution)/shard_map/while/body/eval_jaxpr/ppermute | solution.py:17
  13.6 8.1 %collective-permute-start.2 = (f32[2,192,1,128]{3,1,2,0:T(8,128)S(1)}, f32[2,192,1,128]{3,1,2,0:T(8,128)S(1)}, u32[]{:S(2)}, u32[]{:S(2)}) collective-permute-start(f32[2,192,1,128]{3,1,2,0:T(8,128)S(1)} %get-tuple-element.386), channel_id=1, source_target_pairs={{0,4},{4,8},{8,12},{1,5},{5,9},{9,13},{2,6},{6,10},{10,14},{3,7},{... | collective-permute-start | bytes 589832 | tf_op jit(solution)/shard_map/while/body/eval_jaxpr/ppermute | solution.py:14
  22.1 4.8 %copy-start = (f32[27,192,192]{2,1,0:T(8,128)S(1)}, f32[27,192,192]{2,1,0:T(8,128)}, u32[]{:S(2)}) copy-start(f32[27,192,192]{2,1,0:T(8,128)} %get-tuple-element.219) | copy-start | bytes 11943940 | tf_op jit(solution)/shard_map/while/body/eval_jaxpr/cond
  41.8 2.6 %collective-permute-start = (f32[2,192,2,128]{3,1,2,0:T(8,128)S(1)}, f32[2,192,2,128]{3,1,2,0:T(8,128)S(1)}, u32[]{:S(2)}, u32[]{:S(2)}) collective-permute-start(f32[2,192,2,128]{3,1,2,0:T(8,128)S(1)} %broadcast_select_fusion.7), channel_id=1, source_target_pairs={{0,1},{1,2},{2,3},{4,5},{5,6},{6,7},{8,9},{9,10},{10,11},{12,13},{... | collective-permute-start | bytes 1179656 | tf_op jit(solution)/shard_map/while/body/eval_jaxpr/ppermute | solution.py:25
  45.4 9.8 %collective-permute-start.1 = (f32[2,192,1,128]{3,1,2,0:T(8,128)S(1)}, f32[2,192,1,128]{3,1,2,0:T(8,128)S(1)}, u32[]{:S(2)}, u32[]{:S(2)}) collective-permute-start(f32[2,192,1,128]{3,1,2,0:T(8,128)S(1)} %get-tuple-element.385), channel_id=1, source_target_pairs={{4,0},{8,4},{12,8},{5,1},{9,5},{13,9},{6,2},{10,6},{14,10},{7,3},{... | collective-permute-start | bytes 589832 | tf_op jit(solution)/shard_map/while/body/eval_jaxpr/ppermute | solution.py:17
  46.7 9.7 %collective-permute-start.2 = (f32[2,192,1,128]{3,1,2,0:T(8,128)S(1)}, f32[2,192,1,128]{3,1,2,0:T(8,128)S(1)}, u32[]{:S(2)}, u32[]{:S(2)}) collective-permute-start(f32[2,192,1,128]{3,1,2,0:T(8,128)S(1)} %get-tuple-element.386), channel_id=1, source_target_pairs={{0,4},{4,8},{8,12},{1,5},{5,9},{9,13},{2,6},{6,10},{10,14},{3,7},{... | collective-permute-start | bytes 589832 | tf_op jit(solution)/shard_map/while/body/eval_jaxpr/ppermute | solution.py:14
  57.1 22.1 %collective-permute-start = (f32[2,192,2,128]{3,1,2,0:T(8,128)S(1)}, f32[2,192,2,128]{3,1,2,0:T(8,128)S(1)}, u32[]{:S(2)}, u32[]{:S(2)}) collective-permute-start(f32[2,192,2,128]{3,1,2,0:T(8,128)S(1)} %broadcast_select_fusion.7), channel_id=1, source_target_pairs={{0,1},{1,2},{2,3},{4,5},{5,6},{6,7},{8,9},{9,10},{10,11},{12,13},{... | collective-permute-start | bytes 1179656 | tf_op jit(solution)/shard_map/while/body/eval_jaxpr/ppermute | solution.py:25
  80.2 8.0 %collective-permute-start.1 = (f32[2,192,1,128]{3,1,2,0:T(8,128)S(1)}, f32[2,192,1,128]{3,1,2,0:T(8,128)S(1)}, u32[]{:S(2)}, u32[]{:S(2)}) collective-permute-start(f32[2,192,1,128]{3,1,2,0:T(8,128)S(1)} %get-tuple-element.385), channel_id=1, source_target_pairs={{4,0},{8,4},{12,8},{5,1},{9,5},{13,9},{6,2},{10,6},{14,10},{7,3},{... | collective-permute-start | bytes 589832 | tf_op jit(solution)/shard_map/while/body/eval_jaxpr/ppermute | solution.py:17
  81.5 8.2 %collective-permute-start.2 = (f32[2,192,1,128]{3,1,2,0:T(8,128)S(1)}, f32[2,192,1,128]{3,1,2,0:T(8,128)S(1)}, u32[]{:S(2)}, u32[]{:S(2)}) collective-permute-start(f32[2,192,1,128]{3,1,2,0:T(8,128)S(1)} %get-tuple-element.386), channel_id=1, source_target_pairs={{0,4},{4,8},{8,12},{1,5},{5,9},{9,13},{2,6},{6,10},{10,14},{3,7},{... | collective-permute-start | bytes 589832 | tf_op jit(solution)/shard_map/while/body/eval_jaxpr/ppermute | solution.py:14
  90.4 5.8 %collective-permute-start = (f32[2,192,2,128]{3,1,2,0:T(8,128)S(1)}, f32[2,192,2,128]{3,1,2,0:T(8,128)S(1)}, u32[]{:S(2)}, u32[]{:S(2)}) collective-permute-start(f32[2,192,2,128]{3,1,2,0:T(8,128)S(1)} %broadcast_select_fusion.7), channel_id=1, source_target_pairs={{0,1},{1,2},{2,3},{4,5},{5,6},{6,7},{8,9},{9,10},{10,11},{12,13},{... | collective-permute-start | bytes 1179656 | tf_op jit(solution)/shard_map/while/body/eval_jaxpr/ppermute | solution.py:25
  97.1 7.7 %collective-permute-start.1 = (f32[2,192,1,128]{3,1,2,0:T(8,128)S(1)}, f32[2,192,1,128]{3,1,2,0:T(8,128)S(1)}, u32[]{:S(2)}, u32[]{:S(2)}) collective-permute-start(f32[2,192,1,128]{3,1,2,0:T(8,128)S(1)} %get-tuple-element.385), channel_id=1, source_target_pairs={{4,0},{8,4},{12,8},{5,1},{9,5},{13,9},{6,2},{10,6},{14,10},{7,3},{... | collective-permute-start | bytes 589832 | tf_op jit(solution)/shard_map/while/body/eval_jaxpr/ppermute | solution.py:17
  98.4 7.9 %collective-permute-start.2 = (f32[2,192,1,128]{3,1,2,0:T(8,128)S(1)}, f32[2,192,1,128]{3,1,2,0:T(8,128)S(1)}, u32[]{:S(2)}, u32[]{:S(2)}) collective-permute-start(f32[2,192,1,128]{3,1,2,0:T(8,128)S(1)} %get-tuple-element.386), channel_id=1, source_target_pairs={{0,4},{4,8},{8,12},{1,5},{5,9},{9,13},{2,6},{6,10},{10,14},{3,7},{... | collective-permute-start | bytes 589832 | tf_op jit(solution)/shard_map/while/body/eval_jaxpr/ppermute | solution.py:14
Sparse Core Ops, SparseCore 0:
  107.9 62.3 all-gather.2
